TPU v7x, 512 devices: a whole 4x8x8 slice. The times are simulated.
512 devices in a mesh: dp: 16 (over z, core), head: 8 (over y), tok: 4 (over x).
Axes of the slice: x: 4, y: 8, z: 8, core: 2. Of those that a mesh axis runs over, the one named last changes fastest.
Arguments:
- mamba_input: bfloat16 [32, 64, 8192], P('dp', 'tok', 'head'), may hold values from -6 to 6
- gate_input: bfloat16 [32, 64, 8192], P('dp', 'tok', 'head'), may hold values from -6 to 6
- in_b: bfloat16 [32, 64, 1024], P('dp', 'tok', 'head'), may hold values from -0.75 to 0.75
- in_c: bfloat16 [32, 64, 1024], P('dp', 'tok', 'head'), may hold values from -0.75 to 0.75
- step_size: bfloat16 [32, 64, 128], P('dp', 'tok', 'head'), may hold values from 0.019897461 to 1
- decay_rate: float32 [128], P('head'), may hold values from 0.01 to 1
- skip_weight: float32 [128], P('head'), may hold values from 0.5 to 1.5
- norm_gain: float32 [8192], P('head'), may hold values from 0.1 to 1.9
- ssm_state: bfloat16 [32, 128, 64, 128], P('dp', 'head', None, 'tok'), may hold values from -6 to 6
- out_weight: bfloat16 [8192, 4096], P(('head', 'tok')), may hold values from -0.0625 to 0.0625
- queries: bfloat16 [32, 64, 4096], P('dp', 'tok', 'head'), may hold values from -6 to 6
- draft_token_keys: bfloat16 [32, 64, 1024], P('dp', 'tok', 'head'), may hold values from -6 to 6
- draft_values: bfloat16 [32, 64, 1024], P('dp', 'tok', 'head'), may hold values from -6 to 6
- cached_key_rows: bfloat16 [32, 4096, 1024], P('dp', 'tok', 'head'), may hold values from -4 to 4
- cache_values: bfloat16 [32, 4096, 1024], P('dp', 'tok', 'head'), may hold values from -6 to 6
- cache_len: int32 [32], P('dp'), may hold values from 2 to 4096
- accepted: int32 [32], P('dp'), may hold values from 0 to 64
Outputs:
- mamba_out: bfloat16 [64, 32, 4096], P(('head', 'tok'), 'dp')
- attn_context: bfloat16 [32, 64, 4096], P('dp', 'tok', 'head')
- committed_state: bfloat16 [32, 128, 64, 128], P('dp', 'head', None, 'tok')
Inputs may be any that keep to these rules, and one draw needn't show every extreme that they name: Each sequence's cached positions 0 to cache_len - 1 are valid.
All inputs are finite; a program needn't handle non-finite values.
Results may differ from a plain program's by a relative error of at most 0.018.
Values may be sent and summed in bfloat16 or wider, within the bound.
No kernel may reach another device: no remote copies, remote signals or barrier semaphores. Data moves between devices by JAX's collectives and lax.ppermute only.
A program may use at most 64 MiB of HBM per device.

v0:
```python
import jax
import jax.numpy as jnp
from jax import lax
from jax.sharding import PartitionSpec as P

EPSILON = 1e-05
MASKED = -1e30


def in_one_piece(arrays, axis, split_dim, concat_dim, along):
    widths = [a.shape[along] for a in arrays]
    both = jnp.concatenate(arrays, axis=along)
    filled = lax.all_to_all(both, axis, split_axis=split_dim, concat_axis=concat_dim, tiled=True)
    return tuple(jnp.split(filled, [sum(widths[:k]) for k in range(1, len(widths))], axis=along))


def sent_together(arrays, axis, dim, along):
    widths = [a.shape[along] for a in arrays]
    both = jnp.concatenate(arrays, axis=along)
    filled = lax.all_gather(both, axis, axis=dim, tiled=True)
    return tuple(jnp.split(filled, [sum(widths[:k]) for k in range(1, len(widths))], axis=along))


def in_blocks(array, dim, count):
    before, after = (array.shape[:dim], array.shape[dim + 1 :])
    return jnp.moveaxis(array.reshape(*before, count, -1, *after), dim, 0)


def summed_on_arrival(array, axis, dim):
    parts = in_blocks(array, dim, lax.axis_size(axis))
    arrived = lax.all_to_all(parts, axis, split_axis=0, concat_axis=0, tiled=True)
    return arrived.astype(jnp.float32).sum(axis=0)


def from_everyone(array, axis):
    copies = jnp.broadcast_to(array, (lax.axis_size(axis), *array.shape))
    return lax.all_to_all(copies, axis, split_axis=0, concat_axis=0, tiled=True)


def laid_out(parts, dim):
    parts = jnp.moveaxis(parts, 0, dim)
    shape = parts.shape
    return parts.reshape(*shape[:dim], shape[dim] * shape[dim + 1], *shape[dim + 2 :])


def gather_directly(array, axis, dim):
    parts = from_everyone(array, axis)
    return laid_out(parts, dim)


def within_block(running, step_sizes, feature_values, inflow, readout):
    count = running.shape[1]
    position = jnp.arange(count)
    causal = (position[:, None] >= position[None, :])[None, :, :, None]
    log_gaps = jnp.where(causal, running[:, :, None, :] - running[:, None, :, :], 0.0)
    decays = jnp.where(causal, jnp.exp(log_gaps), 0.0)
    affinity = jnp.einsum("bsn,brn->bsr", readout, inflow)
    mixing = affinity[..., None] * decays * step_sizes[:, None, :, :]
    return jnp.einsum("bsrh,brhp->bshp", mixing, feature_values)


def select_state(limit, log_decay, running, step_sizes, feature_values, inflow, start_state):
    count = running.shape[1]
    alive = (jnp.arange(count)[None, :] < limit[:, None])[..., None]
    end_log = jnp.sum(jnp.where(alive, log_decay, 0.0), axis=1)
    weights = jnp.where(
        alive, jnp.exp(jnp.where(alive, end_log[:, None, :] - running, 0.0)) * step_sizes, 0.0
    )
    return jnp.exp(end_log)[..., None, None] * start_state + jnp.einsum(
        "brh,brhp,brn->bhpn", weights, feature_values, inflow
    )


def body(
    mamba_input,
    gate_input,
    in_b,
    in_c,
    step_size,
    decay_rate,
    skip_weight,
    norm_gain,
    ssm_state,
    out_weight,
    queries,
    draft_token_keys,
    draft_values,
    cached_key_rows,
    cache_values,
    cache_len,
    accepted,
):
    sequences, block_len, feature_width = mamba_input.shape
    head_count = decay_rate.shape[0]
    head_size = feature_width // head_count
    tok_count = lax.axis_size("tok")
    tok_index = lax.axis_index("tok")
    first_draft = tok_index * block_len
    feature_values = mamba_input.astype(jnp.float32).reshape(
        sequences, block_len, head_count, head_size
    )
    inflow_cols, readout_cols = in_one_piece((in_b, in_c), "tok", 2, 1, 0)
    all_inputs, all_steps = sent_together((mamba_input, step_size), "tok", 1, 2)
    draft_len = all_inputs.shape[1]
    all_features = all_inputs.astype(jnp.float32).reshape(
        sequences, draft_len, head_count, head_size
    )
    step_sizes = all_steps.astype(jnp.float32)
    inflow = inflow_cols.astype(jnp.float32)
    readout = readout_cols.astype(jnp.float32)
    log_decay = -step_sizes * decay_rate[None, None, :]
    running = jnp.cumsum(log_decay, axis=1)
    within = within_block(running, step_sizes, all_features, inflow, readout)
    start_state = ssm_state.astype(jnp.float32)
    carried = jnp.einsum("bsn,bhpn->bshp", readout, start_state) * jnp.exp(running)[..., None]
    partial_sum = (within + carried).reshape(sequences, draft_len, feature_width)
    mixed = summed_on_arrival(partial_sum.astype(jnp.bfloat16), "tok", 1).reshape(
        sequences, block_len, head_count, head_size
    )
    chosen = select_state(
        accepted, log_decay, running, step_sizes, all_features, inflow, start_state
    )
    committed_state = chosen.astype(jnp.bfloat16)
    mixed = mixed + skip_weight[None, None, :, None] * feature_values
    gated = mixed.reshape(sequences, block_len, feature_width) * jax.nn.silu(
        gate_input.astype(jnp.float32)
    )
    mean_sq = jnp.mean(gated * gated, axis=-1, keepdims=True)
    normed = (gated * lax.rsqrt(mean_sq + EPSILON) * norm_gain).astype(jnp.bfloat16)
    regrouped = lax.all_to_all(normed, "tok", split_axis=2, concat_axis=1, tiled=True)
    mamba_out = summed_on_arrival(
        jnp.einsum("sdf,fo->dso", regrouped, out_weight, preferred_element_type=jnp.float32).astype(
            jnp.bfloat16
        ),
        ("head", "tok"),
        0,
    ).astype(jnp.bfloat16)
    all_queries = gather_directly(queries, "tok", 1)
    att_size = draft_token_keys.shape[2]
    per_kv = queries.shape[2] // att_size
    draft_len = all_queries.shape[1]
    cache_block = cached_key_rows.shape[1]
    query_matrix = all_queries.reshape(sequences, draft_len * per_kv, att_size)
    score_scale = att_size ** (-0.5)
    cache_scores = (
        jnp.einsum(
            "cmq,czq->cmz", query_matrix, cached_key_rows, preferred_element_type=jnp.float32
        )
        * score_scale
    )
    draft_scores = (
        jnp.einsum(
            "cmq,czq->cmz", query_matrix, draft_token_keys, preferred_element_type=jnp.float32
        )
        * score_scale
    )
    cache_pos = tok_index * cache_block + jnp.arange(cache_block)
    cache_valid = cache_pos[None, None, :] < cache_len[:, None, None]
    query_pos = jnp.repeat(jnp.arange(draft_len), per_kv)
    draft_valid = ((first_draft + jnp.arange(block_len))[None, :] <= query_pos[:, None])[None, :, :]
    cache_scores = jnp.where(cache_valid, cache_scores, MASKED)
    draft_scores = jnp.where(draft_valid, draft_scores, MASKED)
    row_peak = jnp.maximum(jnp.max(cache_scores, axis=-1), jnp.max(draft_scores, axis=-1))
    cache_probs = jnp.where(cache_valid, jnp.exp(cache_scores - row_peak[..., None]), 0.0)
    draft_probs = jnp.where(draft_valid, jnp.exp(draft_scores - row_peak[..., None]), 0.0)
    row_total = jnp.sum(cache_probs, axis=-1) + jnp.sum(draft_probs, axis=-1)
    numer = jnp.einsum(
        "ces,csx->cex",
        cache_probs.astype(jnp.bfloat16),
        cache_values,
        preferred_element_type=jnp.float32,
    )
    numer = numer + jnp.einsum(
        "ces,csx->cex",
        draft_probs.astype(jnp.bfloat16),
        draft_values,
        preferred_element_type=jnp.float32,
    )
    peaks, totals, numers = tuple(
        (
            part.astype(jnp.float32)
            for part in in_one_piece(
                (
                    row_peak.reshape(1, sequences, draft_len, per_kv).astype(jnp.bfloat16),
                    row_total.reshape(1, sequences, draft_len, per_kv).astype(jnp.bfloat16),
                    numer.reshape(1, sequences, draft_len, per_kv * att_size).astype(jnp.bfloat16),
                ),
                "tok",
                2,
                0,
                3,
            )
        )
    )
    overall = jnp.max(peaks, axis=0)
    rescale = jnp.exp(peaks - overall[None])
    denominator = jnp.sum(rescale * totals, axis=0)
    numers = numers.reshape(tok_count, sequences, block_len, per_kv, att_size)
    context = jnp.sum(rescale[..., None] * numers, axis=0) / denominator[..., None]
    attn_context = context.reshape(sequences, block_len, per_kv * att_size).astype(jnp.bfloat16)
    return (mamba_out, attn_context, committed_state)


def solution(mesh):
    in_specs = (
        P("dp", "tok", "head"),
        P("dp", "tok", "head"),
        P("dp", "tok", "head"),
        P("dp", "tok", "head"),
        P("dp", "tok", "head"),
        P("head"),
        P("head"),
        P("head"),
        P("dp", "head", None, "tok"),
        P(("head", "tok"), None),
        P("dp", "tok", "head"),
        P("dp", "tok", "head"),
        P("dp", "tok", "head"),
        P("dp", "tok", "head"),
        P("dp", "tok", "head"),
        P("dp"),
        P("dp"),
    )
    out_specs = (
        P(("head", "tok"), "dp", None),
        P("dp", "tok", "head"),
        P("dp", "head", None, "tok"),
    )
    return jax.shard_map(body, mesh=mesh, in_specs=in_specs, out_specs=out_specs, check_vma=False)
```

profile of v0, /device:TPU:450, one launch (start us, length us, event | category | flops | bytes accessed | tf_op | source)
XLA Modules:
  0.0 98.2 jit_solution(13853714180560108559)
XLA Ops:
  0.7 0.9 pad_maximum_fusion.2
  1.5 0.1 copy.76
  1.7 0.8 reshape.233
  2.4 4.8 %all-to-all-start = ((bf16[4,2,1024]{2,1,0:T(2,128)(2,1)}), bf16[4,2,1024]{2,1,0:T(2,128)(2,1)S(1)}, u32[]{:S(2)}, u32[]{:S(2)}) async-start(bf16[4,2,1024]{2,1,0:T(2,128)(2,1)} %reshape.233), calls=%async_computation | async-start | bytes 32768 | tf_op jit(solution)/shard_map/all_to_all | solution.py:13
  7.4 0.9 pad_maximum_fusion.1
  8.3 12.6 %all_gather.3 = bf16[2,64,1040]{2,1,0:T(8,128)(2,1)S(1)} all-gather(bf16[2,16,1040]{2,1,0:T(8,128)(2,1)S(1)} %pad_maximum_fusion.1), channel_id=1, replica_groups=mesh['dp'=16,'head'=8,'tok'=4] {'tok'}, dimensions={1}, use_global_device_ids=true | all-gather | bytes 332800 | tf_op jit(solution)/shard_map/all_gather | solution.py:20
  20.9 0.7 iota_compare_fusion.1
  21.6 0.7 broadcast_compare_fusion.1
  22.4 0.8 select_reduce_fusion
  23.5 0.3 copy.75
  24.1 0.7 broadcast_in_dim.109
  24.8 4.5 %all-to-all-start.4 = ((bf16[4,2,16,512]{3,2,1,0:T(8,128)(2,1)}), bf16[4,2,16,512]{3,2,1,0:T(8,128)(2,1)S(1)}, u32[]{:S(2)}, u32[]{:S(2)}) async-start(bf16[4,2,16,512]{3,2,1,0:T(8,128)(2,1)} %broadcast_in_dim.109), calls=%async_computation.4 | async-start | bytes 262144 | tf_op jit(solution)/shard_map/all_to_all | solution.py:37
  29.3 0.1 reshape.234
  29.4 0.1 copy.77
  29.7 0.5 convolution_bitcast_fusion
  30.2 1.3 %fusion.6 = bf16[2,64,16,64]{1,3,2,0:T(8,128)(2,1)S(1)} fusion(f32[2,64,16,64]{1,3,2,0:T(8,128)S(1)} %convolution_bitcast_fusion, bf16[2,64,32,1]{2,1,3,0:T(8,128)(2,1)S(1)} %bitcast.67, bf16[2,16,64,32]{2,3,1,0:T(8,128)(2,1)} %param.25, f32[2,64,16]{1,2,0:T(8,128)S(1)} %copy.84), kind=kOutput, calls=%fused_computation.11 | convolution fusion | flops 8781824 | bytes 933888 | tf_op jit(solution)/shard_map/bsn,bhpn->bshp/dot_general | solution.py:115
  31.5 0.4 copy.86
  31.9 0.3 convert_element_type.101
  32.3 0.7 copy.87
  33.0 0.7 all-to-all-done.4
  33.8 4.8 %all-to-all-start.1 = ((bf16[4,2,16,1024]{3,2,1,0:T(8,128)(2,1)}), bf16[4,2,16,1024]{3,2,1,0:T(8,128)(2,1)S(1)}, u32[]{:S(2)}, u32[]{:S(2)}) async-start(bf16[4,2,16,1024]{3,2,1,0:T(8,128)(2,1)} %copy.87), calls=%async_computation.1 | async-start | bytes 524288 | tf_op jit(solution)/shard_map/all_to_all | solution.py:31
  38.7 1.6 %fusion.2 = (f32[2,256]{1,0:T(2,128)S(1)}, f32[2,256,1024]{2,1,0:T(8,128)S(1)}) fusion(pred[2,1024]{1,0:T(4,128)(4,1)S(1)} %broadcast_compare_fusion.1, bf16[2,256,128]{2,1,0:T(8,128)(2,1)S(1)} %reshape_reshape.3, bf16[2,1024,128]{2,1,0:T(8,128)(2,1)} %param.30), kind=kOutput, calls=%fused_computation.5 | convolution fusion | flops 135790080 | bytes 2756608 | tf_op jit(solution)/shard_map/cmq,czq->cmz/dot_general | solution.py:146
  40.4 0.2 fusion.49
  40.6 0.2 fusion.36
  40.8 0.6 fusion.4
  41.5 0.7 fusion.8
  42.3 0.1 copy.95
  42.8 1.1 %all-to-all-done.1 = bf16[4,2,16,1024]{3,2,1,0:T(8,128)(2,1)S(1)} async-done(((bf16[4,2,16,1024]{3,2,1,0:T(8,128)(2,1)}), bf16[4,2,16,1024]{3,2,1,0:T(8,128)(2,1)S(1)}, u32[]{:S(2)}, u32[]{:S(2)}) %all-to-all-start.1) | async-done | bytes 262176 | tf_op jit(solution)/shard_map/all_to_all | solution.py:31
  44.1 0.4 copy.88
  44.5 1.2 %reshape.235 = bf16[4,2,4096]{2,1,0:T(2,128)(2,1)} reshape(bf16[1024,2,16]{2,1,0:T(2,128)(2,1)S(1)} %bitcast.55) | data formatting | bytes 131072
  45.7 4.7 %all-to-all-start.2 = ((bf16[4,2,4096]{2,1,0:T(2,128)(2,1)}), bf16[4,2,4096]{2,1,0:T(2,128)(2,1)S(1)}, u32[]{:S(2)}, u32[]{:S(2)}) async-start(bf16[4,2,4096]{2,1,0:T(2,128)(2,1)} %reshape.235), calls=%async_computation.2 | async-start | bytes 131072 | tf_op jit(solution)/shard_map/all_to_all | solution.py:130
  50.4 1.1 %pad_maximum_fusion = bf16[1,2,64,520]{3,1,0,2:T(2,128)(2,1)} fusion(bf16[1,2,64,512]{3,1,0,2:T(2,128)(2,1)S(1)} %copy.95, bf16[1,2,64,4]{3,1,0,2:T(2,128)(2,1)S(1)} %copy.94, bf16[1,2,64,4]{3,1,0,2:T(2,128)(2,1)S(1)} %copy.93), kind=kLoop, calls=%fused_computation.41 | loop fusion | flops 399360 | bytes 266240 | tf_op jit(solution)/shard_map/concatenate | solution.py:12
  51.5 3.1 %all-to-all-done.2 = bf16[4,2,4096]{2,1,0:T(2,128)(2,1)S(1)} async-done(((bf16[4,2,4096]{2,1,0:T(2,128)(2,1)}), bf16[4,2,4096]{2,1,0:T(2,128)(2,1)S(1)}, u32[]{:S(2)}, u32[]{:S(2)}) %all-to-all-start.2) | async-done | bytes 65568 | tf_op jit(solution)/shard_map/all_to_all | solution.py:130
  54.6 4.8 %all-to-all-start.5 = ((bf16[1,2,64,520]{3,1,0,2:T(2,128)(2,1)}), bf16[1,2,64,520]{3,1,0,2:T(2,128)(2,1)S(1)}, u32[]{:S(2)}, u32[]{:S(2)}) async-start(bf16[1,2,64,520]{3,1,0,2:T(2,128)(2,1)} %pad_maximum_fusion), calls=%async_computation.5 | async-start | bytes 327680 | tf_op jit(solution)/shard_map/all_to_all | solution.py:13
  59.3 0.4 reshape.236
  59.7 0.3 copy.89
  60.1 0.4 fusion
  60.5 1.5 %reshape.230 = bf16[32,2,2,4096]{3,1,0,2:T(2,128)(2,1)} reshape(bf16[64,2,4096]{2,0,1:T(8,128)(2,1)S(1)} %fusion) | data formatting | bytes 2097152 | tf_op jit(solution)/shard_map/reshape | solution.py:26
  62.0 3.4 %copy.90 = bf16[32,2,2,4096]{3,1,2,0:T(2,128)(2,1)} copy(bf16[32,2,2,4096]{3,1,0,2:T(2,128)(2,1)} %reshape.230) | data formatting | bytes 2097152 | tf_op jit(solution)/shard_map/reshape | solution.py:26
  65.4 10.2 %all-to-all-start.3 = ((bf16[32,2,2,4096]{3,1,2,0:T(2,128)(2,1)}), bf16[32,2,2,4096]{3,1,2,0:T(2,128)(2,1)S(1)}, u32[]{:S(2)}, u32[]{:S(2)}) async-start(bf16[32,2,2,4096]{3,1,2,0:T(2,128)(2,1)} %copy.90), calls=%async_computation.3 | async-start | bytes 2097152 | tf_op jit(solution)/shard_map/all_to_all | solution.py:31
  75.8 2.2 %fusion.7 = bf16[2,16,64,32]{2,3,1,0:T(8,128)(2,1)} fusion(bf16[2,64,16,64]{1,3,2,0:T(8,128)(2,1)} %bitcast.62, bf16[2,16,64,32]{2,3,1,0:T(8,128)(2,1)} %param.25, f32[2,64,16]{1,2,0:T(8,128)S(1)} %copy.97, f32[2,64,32]{1,2,0:T(8,128)S(1)} %copy.96, f32[2,16]{1,0:T(2,128)S(1)} %exp.39), kind=kOutput, calls=%fused_computation.13 | convolution fusion | flops 8716288 | bytes 548992 | tf_op jit(solution)/shard_map/brh,brhp,brn->bhpn/dot_general | solution.py:69
  78.3 0.9 mul.139
  79.2 1.1 %mul.140 = f32[4,2,16,512]{3,1,2,0:T(2,128)S(1)} reshape(f32[4,2,16,4,128]{4,3,1,2,0:T(4,128)} %mul.139) | data formatting | bytes 524288 | tf_op jit(solution)/shard_map/mul | solution.py:199
  80.5 1.2 %multiply_reduce_fusion = f32[2,16,512]{2,0,1:T(2,128)S(1)} fusion(f32[4,2,16,512]{3,1,2,0:T(2,128)S(1)} %mul.140, bf16[4,2,16,520]{3,1,2,0:T(2,128)(2,1)} %bitcast.60), kind=kLoop, calls=%fused_computation.38 | loop fusion | flops 180224 | bytes 458752 | tf_op jit(solution)/shard_map/reduce_sum | solution.py:199
  81.8 0.6 copy.100
  82.4 14.1 %all-to-all-done.3 = bf16[32,2,2,4096]{3,1,2,0:T(2,128)(2,1)S(1)} async-done(((bf16[32,2,2,4096]{3,1,2,0:T(2,128)(2,1)}), bf16[32,2,2,4096]{3,1,2,0:T(2,128)(2,1)S(1)}, u32[]{:S(2)}, u32[]{:S(2)}) %all-to-all-start.3) | async-done | bytes 1048608 | tf_op jit(solution)/shard_map/all_to_all | solution.py:31
  96.5 1.0 %reduce_sum.77 = bf16[2,2,4096]{2,0,1:T(2,128)(2,1)S(1)} reduce(bf16[32,2,2,4096]{3,1,2,0:T(2,128)(2,1)S(1)} %all-to-all-done.3, bf16[]{:T(256)} %constant.10.clone.1), dimensions={0}, to_apply=%region_3.4 | reduce | flops 507904 | bytes 1081346 | tf_op jit(solution)/shard_map/reduce_sum | solution.py:32
  97.5 0.7 copy.99
  (65 shorter events, 2.3 us)
Async XLA Ops:
  0.6 59.4 %copy-start = (bf16[256,4096]{1,0:T(8,128)(2,1)S(1)}, bf16[256,4096]{1,0:T(8,128)(2,1)}, u32[]{:S(2)}) copy-start(bf16[256,4096]{1,0:T(8,128)(2,1)} %param.26) | copy-start | bytes 6291460
  0.6 23.3 %copy-start.9 = (f32[16]{0:T(128)S(1)}, f32[16]{0:T(128)}, u32[]{:S(2)}) copy-start(f32[16]{0:T(128)} %param.23) | copy-start | bytes 196
  0.7 23.4 %copy-start.5 = (bf16[2,16,512]{2,1,0:T(8,128)(2,1)S(1)}, bf16[2,16,512]{2,1,0:T(8,128)(2,1)}, u32[]{:S(2)}) copy-start(bf16[2,16,512]{2,1,0:T(8,128)(2,1)} %param.27) | copy-start | bytes 98308
  2.4 21.6 %all-to-all-start = ((bf16[4,2,1024]{2,1,0:T(2,128)(2,1)}), bf16[4,2,1024]{2,1,0:T(2,128)(2,1)S(1)}, u32[]{:S(2)}, u32[]{:S(2)}) async-start(bf16[4,2,1024]{2,1,0:T(2,128)(2,1)} %reshape.233), calls=%async_computation | async-start | bytes 32768 | tf_op jit(solution)/shard_map/all_to_all | solution.py:13
  23.8 6.4 %copy-start.2 = (bf16[2,64,1024]{1,2,0:T(8,128)(2,1)}, bf16[2,64,1024]{1,2,0:T(8,128)(2,1)S(1)}, u32[]{:S(2)}) copy-start(bf16[2,64,1024]{1,2,0:T(8,128)(2,1)S(1)} %copy.75) | copy-start | bytes 786436
  24.8 9.0 %all-to-all-start.4 = ((bf16[4,2,16,512]{3,2,1,0:T(8,128)(2,1)}), bf16[4,2,16,512]{3,2,1,0:T(8,128)(2,1)S(1)}, u32[]{:S(2)}, u32[]{:S(2)}) async-start(bf16[4,2,16,512]{3,2,1,0:T(8,128)(2,1)} %broadcast_in_dim.109), calls=%async_computation.4 | async-start | bytes 262144 | tf_op jit(solution)/shard_map/all_to_all | solution.py:37
  32.3 8.1 %copy-start.6 = (bf16[2,16,128]{2,1,0:T(8,128)(2,1)S(1)}, bf16[2,16,128]{2,1,0:T(8,128)(2,1)}, u32[]{:S(2)}) copy-start(bf16[2,16,128]{2,1,0:T(8,128)(2,1)} %param.28) | copy-start | bytes 24580
  33.0 7.6 %copy-start.7 = (bf16[2,16,128]{2,1,0:T(8,128)(2,1)S(1)}, bf16[2,16,128]{2,1,0:T(8,128)(2,1)}, u32[]{:S(2)}) copy-start(bf16[2,16,128]{2,1,0:T(8,128)(2,1)} %param.29) | copy-start | bytes 24580
  33.8 10.1 %all-to-all-start.1 = ((bf16[4,2,16,1024]{3,2,1,0:T(8,128)(2,1)}), bf16[4,2,16,1024]{3,2,1,0:T(8,128)(2,1)S(1)}, u32[]{:S(2)}, u32[]{:S(2)}) async-start(bf16[4,2,16,1024]{3,2,1,0:T(8,128)(2,1)} %copy.87), calls=%async_computation.1 | async-start | bytes 524288 | tf_op jit(solution)/shard_map/all_to_all | solution.py:31
  38.7 2.8 %copy-start.10 = (bf16[2,1024,128]{2,1,0:T(8,128)(2,1)S(1)}, bf16[2,1024,128]{2,1,0:T(8,128)(2,1)}, u32[]{:S(2)}) copy-start(bf16[2,1024,128]{2,1,0:T(8,128)(2,1)} %param.31) | copy-start | bytes 1572868
  41.5 2.4 %copy-start.3 = (bf16[2,16,1024]{2,1,0:T(8,128)(2,1)S(1)}, bf16[2,16,1024]{2,1,0:T(8,128)(2,1)}, u32[]{:S(2)}) copy-start(bf16[2,16,1024]{2,1,0:T(8,128)(2,1)} %param.17) | copy-start | bytes 196612
  41.5 2.4 %copy-start.4 = (bf16[2,16,1024]{2,1,0:T(8,128)(2,1)S(1)}, bf16[2,16,1024]{2,1,0:T(8,128)(2,1)}, u32[]{:S(2)}) copy-start(bf16[2,16,1024]{2,1,0:T(8,128)(2,1)} %param.18) | copy-start | bytes 196612
  41.5 2.5 %copy-start.8 = (f32[1024]{0:T(1024)S(1)}, f32[1024]{0:T(1024)}, u32[]{:S(2)}) copy-start(f32[1024]{0:T(1024)} %param.24) | copy-start | bytes 12292
  45.7 8.9 %all-to-all-start.2 = ((bf16[4,2,4096]{2,1,0:T(2,128)(2,1)}), bf16[4,2,4096]{2,1,0:T(2,128)(2,1)S(1)}, u32[]{:S(2)}, u32[]{:S(2)}) async-start(bf16[4,2,4096]{2,1,0:T(2,128)(2,1)} %reshape.235), calls=%async_computation.2 | async-start | bytes 131072 | tf_op jit(solution)/shard_map/all_to_all | solution.py:130
  54.6 10.8 %all-to-all-start.5 = ((bf16[1,2,64,520]{3,1,0,2:T(2,128)(2,1)}), bf16[1,2,64,520]{3,1,0,2:T(2,128)(2,1)S(1)}, u32[]{:S(2)}, u32[]{:S(2)}) async-start(bf16[1,2,64,520]{3,1,0,2:T(2,128)(2,1)} %pad_maximum_fusion), calls=%async_computation.5 | async-start | bytes 327680 | tf_op jit(solution)/shard_map/all_to_all | solution.py:13
  65.4 12.8 %copy-start.1 = (bf16[1,2,64,520]{3,1,0,2:T(2,128)(2,1)}, bf16[1,2,64,520]{3,1,0,2:T(2,128)(2,1)S(1)}, u32[]{:S(2)}) copy-start(bf16[1,2,64,520]{3,1,0,2:T(2,128)(2,1)S(1)} %all-to-all-done.5) | copy-start | bytes 399364
  65.4 31.1 %all-to-all-start.3 = ((bf16[32,2,2,4096]{3,1,2,0:T(2,128)(2,1)}), bf16[32,2,2,4096]{3,1,2,0:T(2,128)(2,1)S(1)}, u32[]{:S(2)}, u32[]{:S(2)}) async-start(bf16[32,2,2,4096]{3,1,2,0:T(2,128)(2,1)} %copy.90), calls=%async_computation.3 | async-start | bytes 2097152 | tf_op jit(solution)/shard_map/all_to_all | solution.py:31
where the time goes:
time: 99.1 us; the launch traced here: 98.2 us
  starting transfers between devices  33.9 us (34%)
  waiting for transfers between devices  19 us (19%)
  local copies, waits for them, and re-layouts  15.6 us (16%)
  blocking collectives  12.6 us (13%)
  other arithmetic  8.71 us (9%)
  matrix products  7.29 us (7%)
  between operations  1.06 us (1%)
    all_to_all x2, waiting for transfers between devices, summed_on_arrival(): lax.all_to_all(parts, axis, split_axis=0, concat_axis=0, tiled=True)  15.2 us
    all_to_all x2, starting transfers between devices, summed_on_arrival(): lax.all_to_all(parts, axis, split_axis=0, concat_axis=0, tiled=True)  15.1 us
    all_gather x1, blocking collectives, sent_together(): filled = lax.all_gather(both, axis, axis=dim, tiled=True)  12.6 us
    all_to_all x2, starting transfers between devices, in_one_piece(): lax.all_to_all(both, axis, split_axis=split_dim, concat_axis=concat_dim,...  9.59 us
    reshape x2, local copies, waits for them, and re-layouts, in_blocks(): return jnp.moveaxis(array.reshape(*before, count, -1, *after), dim, 0)  4.9 us
    all_to_all x1, starting transfers between devices, body(): lax.all_to_all(normed, 'tok', split_axis=2, concat_axis=1, tiled=True)  4.71 us
    all_to_all x1, starting transfers between devices, from_everyone(): return lax.all_to_all(copies, axis, split_axis=0, concat_axis=0, tiled=True)  4.5 us
    unnamed x28, local copies, waits for them, and re-layouts  3.78 us
  transfers between devices with their start and end apart: 6, of which 4 were waited for; matrix products, arithmetic and copies ran while one was open for 26% of the time, Pallas kernels for 0%

commit v1 on v0

--- a/solution.py
+++ b/solution.py
@@ -90,6 +90,14 @@
     cache_len,
     accepted,
 ):
+
+    def pieces_all_register(vals):
+        v_now = lax.axis_size("tok")
+        x_new = jnp.split(vals, v_now, axis=2)
+        outer = jnp.stack(x_new, axis=0)
+        left_arr = lax.all_to_all(outer, "tok", 0, 0)
+        return jnp.concatenate(left_arr, axis=1)
+
     sequences, block_len, feature_width = mamba_input.shape
     head_count = decay_rate.shape[0]
     head_size = feature_width // head_count
@@ -127,7 +135,7 @@
     )
     mean_sq = jnp.mean(gated * gated, axis=-1, keepdims=True)
     normed = (gated * lax.rsqrt(mean_sq + EPSILON) * norm_gain).astype(jnp.bfloat16)
-    regrouped = lax.all_to_all(normed, "tok", split_axis=2, concat_axis=1, tiled=True)
+    regrouped = pieces_all_register(normed)
     mamba_out = summed_on_arrival(
         jnp.einsum("sdf,fo->dso", regrouped, out_weight, preferred_element_type=jnp.float32).astype(
             jnp.bfloat16

time: 99.1 us -> 97.5 us (0.984)
  the two profiles are of different devices: /device:TPU:450 before, /device:TPU:194 now
where the time goes in v1:
time: 97.5 us; the launch traced here: 96.5 us
  starting transfers between devices  33.9 us (35%)
  waiting for transfers between devices  19 us (19%)
  local copies, waits for them, and re-layouts  13.3 us (14%)
  blocking collectives  12.6 us (13%)
  other arithmetic  9.34 us (10%)
  matrix products  7.29 us (7%)
  between operations  1.04 us (1%)
    all_to_all x2, waiting for transfers between devices, summed_on_arrival(): lax.all_to_all(parts, axis, split_axis=0, concat_axis=0, tiled=True)  15.2 us
    all_to_all x2, starting transfers between devices, summed_on_arrival(): lax.all_to_all(parts, axis, split_axis=0, concat_axis=0, tiled=True)  15.1 us
    all_gather x1, blocking collectives, sent_together(): filled = lax.all_gather(both, axis, axis=dim, tiled=True)  12.6 us
    all_to_all x2, starting transfers between devices, in_one_piece(): lax.all_to_all(both, axis, split_axis=split_dim, concat_axis=concat_dim,...  9.59 us
    reshape x2, local copies, waits for them, and re-layouts, in_blocks(): return jnp.moveaxis(array.reshape(*before, count, -1, *after), dim, 0)  4.9 us
    all_to_all x1, starting transfers between devices, pieces_all_register(): left_arr = lax.all_to_all(outer, 'tok', 0, 0)  4.71 us
    all_to_all x1, starting transfers between devices, from_everyone(): return lax.all_to_all(copies, axis, split_axis=0, concat_axis=0, tiled=True)  4.5 us
    all_to_all x1, waiting for transfers between devices, pieces_all_register(): left_arr = lax.all_to_all(outer, 'tok', 0, 0)  3.11 us
  transfers between devices with their start and end apart: 6, of which 4 were waited for; matrix products, arithmetic and copies ran while one was open for 26% of the time, Pallas kernels for 0%

profile of v1, /device:TPU:194, one launch (start us, length us, event | category | flops | bytes accessed | tf_op | source)
XLA Modules:
  0.0 96.5 jit_solution(2423926541989380240)
XLA Ops:
  0.7 0.9 pad_maximum_fusion.3
  1.5 0.1 copy.69
  1.7 0.8 reshape.241
  2.4 4.8 %all-to-all-start = ((bf16[4,2,1024]{2,1,0:T(2,128)(2,1)}), bf16[4,2,1024]{2,1,0:T(2,128)(2,1)S(1)}, u32[]{:S(2)}, u32[]{:S(2)}) async-start(bf16[4,2,1024]{2,1,0:T(2,128)(2,1)} %reshape.241), calls=%async_computation | async-start | bytes 32768 | tf_op jit(solution)/shard_map/all_to_all | solution.py:13
  7.4 0.9 pad_maximum_fusion.1
  8.3 12.6 %all_gather.3 = bf16[2,64,1040]{2,1,0:T(8,128)(2,1)S(1)} all-gather(bf16[2,16,1040]{2,1,0:T(8,128)(2,1)S(1)} %pad_maximum_fusion.1), channel_id=1, replica_groups=mesh['dp'=16,'head'=8,'tok'=4] {'tok'}, dimensions={1}, use_global_device_ids=true | all-gather | bytes 332800 | tf_op jit(solution)/shard_map/all_gather | solution.py:20
  20.9 0.7 iota_compare_fusion.1
  21.6 0.7 broadcast_compare_fusion.1
  22.4 0.8 select_reduce_fusion
  23.5 0.3 copy.68
  24.1 0.7 broadcast_in_dim.109
  24.8 4.5 %all-to-all-start.4 = ((bf16[4,2,16,512]{3,2,1,0:T(8,128)(2,1)}), bf16[4,2,16,512]{3,2,1,0:T(8,128)(2,1)S(1)}, u32[]{:S(2)}, u32[]{:S(2)}) async-start(bf16[4,2,16,512]{3,2,1,0:T(8,128)(2,1)} %broadcast_in_dim.109), calls=%async_computation.4 | async-start | bytes 262144 | tf_op jit(solution)/shard_map/all_to_all | solution.py:37
  29.3 0.1 reshape.242
  29.4 0.1 copy.70
  29.6 0.1 fusion.50
  29.7 0.5 convolution_bitcast_fusion
  30.2 1.3 %fusion.6 = bf16[2,64,16,64]{1,3,2,0:T(8,128)(2,1)S(1)} fusion(f32[2,64,16,64]{1,3,2,0:T(8,128)S(1)} %convolution_bitcast_fusion, bf16[2,64,32,1]{2,1,3,0:T(8,128)(2,1)S(1)} %bitcast.69, bf16[2,16,64,32]{2,3,1,0:T(8,128)(2,1)} %param.25, f32[2,64,16]{1,2,0:T(8,128)S(1)} %copy.77), kind=kOutput, calls=%fused_computation.11 | convolution fusion | flops 8781824 | bytes 933888 | tf_op jit(solution)/shard_map/bsn,bhpn->bshp/dot_general | solution.py:123
  31.5 0.4 copy.79
  31.9 0.3 convert_element_type.101
  32.3 0.7 copy.80
  33.0 0.7 all-to-all-done.4
  33.8 4.8 %all-to-all-start.1 = ((bf16[4,2,16,1024]{3,2,1,0:T(8,128)(2,1)}), bf16[4,2,16,1024]{3,2,1,0:T(8,128)(2,1)S(1)}, u32[]{:S(2)}, u32[]{:S(2)}) async-start(bf16[4,2,16,1024]{3,2,1,0:T(8,128)(2,1)} %copy.80), calls=%async_computation.1 | async-start | bytes 524288 | tf_op jit(solution)/shard_map/all_to_all | solution.py:31
  38.7 1.6 %fusion.2 = (f32[2,256]{1,0:T(2,128)S(1)}, f32[2,256,1024]{2,1,0:T(8,128)S(1)}) fusion(pred[2,1024]{1,0:T(4,128)(4,1)S(1)} %broadcast_compare_fusion.1, bf16[2,256,128]{2,1,0:T(8,128)(2,1)S(1)} %reshape_reshape.3, bf16[2,1024,128]{2,1,0:T(8,128)(2,1)} %param.30), kind=kOutput, calls=%fused_computation.5 | convolution fusion | flops 135790080 | bytes 2756608 | tf_op jit(solution)/shard_map/cmq,czq->cmz/dot_general | solution.py:154
  40.4 0.2 fusion.49
  40.6 0.2 fusion.36
  40.8 0.6 fusion.4
  41.5 0.7 fusion.8
  42.3 0.1 copy.87
  42.8 1.1 %all-to-all-done.1 = bf16[4,2,16,1024]{3,2,1,0:T(8,128)(2,1)S(1)} async-done(((bf16[4,2,16,1024]{3,2,1,0:T(8,128)(2,1)}), bf16[4,2,16,1024]{3,2,1,0:T(8,128)(2,1)S(1)}, u32[]{:S(2)}, u32[]{:S(2)}) %all-to-all-start.1) | async-done | bytes 262176 | tf_op jit(solution)/shard_map/all_to_all | solution.py:31
  43.9 0.1 multiply_reduce_fusion.1
  44.2 0.6 pad_maximum_fusion.2
  44.8 4.7 %all-to-all-start.2 = ((bf16[4,2,16,256]{3,2,1,0:T(8,128)(2,1)}), bf16[4,2,16,256]{3,2,1,0:T(8,128)(2,1)S(1)}, u32[]{:S(2)}, u32[]{:S(2)}) async-start(bf16[4,2,16,256]{3,2,1,0:T(8,128)(2,1)} %pad_maximum_fusion.2), calls=%async_computation.2 | async-start | bytes 131072 | tf_op jit(solution)/shard_map/all_to_all | solution.py:98
  49.5 1.1 %pad_maximum_fusion = bf16[1,2,64,520]{3,1,0,2:T(2,128)(2,1)} fusion(bf16[1,2,64,512]{3,1,0,2:T(2,128)(2,1)S(1)} %copy.87, bf16[1,2,64,4]{3,1,0,2:T(2,128)(2,1)S(1)} %copy.86, bf16[1,2,64,4]{3,1,0,2:T(2,128)(2,1)S(1)} %copy.85), kind=kLoop, calls=%fused_computation.41 | loop fusion | flops 399360 | bytes 266240 | tf_op jit(solution)/shard_map/concatenate | solution.py:12
  50.6 3.1 %all-to-all-done.2 = bf16[4,2,16,256]{3,2,1,0:T(8,128)(2,1)S(1)} async-done(((bf16[4,2,16,256]{3,2,1,0:T(8,128)(2,1)}), bf16[4,2,16,256]{3,2,1,0:T(8,128)(2,1)S(1)}, u32[]{:S(2)}, u32[]{:S(2)}) %all-to-all-start.2) | async-done | bytes 65568 | tf_op jit(solution)/shard_map/all_to_all | solution.py:98
  53.7 4.8 %all-to-all-start.5 = ((bf16[1,2,64,520]{3,1,0,2:T(2,128)(2,1)}), bf16[1,2,64,520]{3,1,0,2:T(2,128)(2,1)S(1)}, u32[]{:S(2)}, u32[]{:S(2)}) async-start(bf16[1,2,64,520]{3,1,0,2:T(2,128)(2,1)} %pad_maximum_fusion), calls=%async_computation.5 | async-start | bytes 327680 | tf_op jit(solution)/shard_map/all_to_all | solution.py:13
  58.5 0.4 fusion
  58.9 1.5 %reshape.238 = bf16[32,2,2,4096]{3,1,0,2:T(2,128)(2,1)} reshape(bf16[64,2,4096]{2,0,1:T(8,128)(2,1)S(1)} %fusion) | data formatting | bytes 2097152 | tf_op jit(solution)/shard_map/reshape | solution.py:26
  60.4 3.4 %copy.82 = bf16[32,2,2,4096]{3,1,2,0:T(2,128)(2,1)} copy(bf16[32,2,2,4096]{3,1,0,2:T(2,128)(2,1)} %reshape.238) | data formatting | bytes 2097152 | tf_op jit(solution)/shard_map/reshape | solution.py:26
  63.8 10.2 %all-to-all-start.3 = ((bf16[32,2,2,4096]{3,1,2,0:T(2,128)(2,1)}), bf16[32,2,2,4096]{3,1,2,0:T(2,128)(2,1)S(1)}, u32[]{:S(2)}, u32[]{:S(2)}) async-start(bf16[32,2,2,4096]{3,1,2,0:T(2,128)(2,1)} %copy.82), calls=%async_computation.3 | async-start | bytes 2097152 | tf_op jit(solution)/shard_map/all_to_all | solution.py:31
  74.2 2.2 %fusion.7 = bf16[2,16,64,32]{2,3,1,0:T(8,128)(2,1)} fusion(bf16[2,64,16,64]{1,3,2,0:T(8,128)(2,1)} %bitcast.64, bf16[2,16,64,32]{2,3,1,0:T(8,128)(2,1)} %param.25, f32[2,64,16]{1,2,0:T(8,128)S(1)} %copy.89, f32[2,64,32]{1,2,0:T(8,128)S(1)} %copy.88, f32[2,16]{1,0:T(2,128)S(1)} %exp.39), kind=kOutput, calls=%fused_computation.13 | convolution fusion | flops 8716288 | bytes 548992 | tf_op jit(solution)/shard_map/brh,brhp,brn->bhpn/dot_general | solution.py:69
  76.5 0.1 multiply_reduce_fusion.2
  76.6 0.9 mul.139
  77.6 1.1 %mul.140 = f32[4,2,16,512]{3,1,2,0:T(2,128)S(1)} reshape(f32[4,2,16,4,128]{4,3,1,2,0:T(4,128)} %mul.139) | data formatting | bytes 524288 | tf_op jit(solution)/shard_map/mul | solution.py:207
  78.9 1.2 %multiply_reduce_fusion = f32[2,16,512]{2,0,1:T(2,128)S(1)} fusion(f32[4,2,16,512]{3,1,2,0:T(2,128)S(1)} %mul.140, bf16[4,2,16,520]{3,1,2,0:T(2,128)(2,1)} %bitcast.62), kind=kLoop, calls=%fused_computation.38 | loop fusion | flops 180224 | bytes 458752 | tf_op jit(solution)/shard_map/reduce_sum | solution.py:207
  80.1 0.6 copy.92
  80.8 14.1 %all-to-all-done.3 = bf16[32,2,2,4096]{3,1,2,0:T(2,128)(2,1)S(1)} async-done(((bf16[32,2,2,4096]{3,1,2,0:T(2,128)(2,1)}), bf16[32,2,2,4096]{3,1,2,0:T(2,128)(2,1)S(1)}, u32[]{:S(2)}, u32[]{:S(2)}) %all-to-all-start.3) | async-done | bytes 1048608 | tf_op jit(solution)/shard_map/all_to_all | solution.py:31
  94.9 1.0 %reduce_sum.77 = bf16[2,2,4096]{2,0,1:T(2,128)(2,1)S(1)} reduce(bf16[32,2,2,4096]{3,1,2,0:T(2,128)(2,1)S(1)} %all-to-all-done.3, bf16[]{:T(256)} %constant.10.clone.1), dimensions={0}, to_apply=%region_3.4 | reduce | flops 507904 | bytes 1081346 | tf_op jit(solution)/shard_map/reduce_sum | solution.py:32
  95.9 0.7 copy.91
  (64 shorter events, 1.9 us)
Async XLA Ops:
  0.6 57.8 %copy-start = (bf16[256,4096]{1,0:T(8,128)(2,1)S(1)}, bf16[256,4096]{1,0:T(8,128)(2,1)}, u32[]{:S(2)}) copy-start(bf16[256,4096]{1,0:T(8,128)(2,1)} %param.26) | copy-start | bytes 6291460
  0.6 23.3 %copy-start.9 = (f32[16]{0:T(128)S(1)}, f32[16]{0:T(128)}, u32[]{:S(2)}) copy-start(f32[16]{0:T(128)} %param.23) | copy-start | bytes 196
  0.7 23.4 %copy-start.5 = (bf16[2,16,512]{2,1,0:T(8,128)(2,1)S(1)}, bf16[2,16,512]{2,1,0:T(8,128)(2,1)}, u32[]{:S(2)}) copy-start(bf16[2,16,512]{2,1,0:T(8,128)(2,1)} %param.27) | copy-start | bytes 98308
  2.4 21.6 %all-to-all-start = ((bf16[4,2,1024]{2,1,0:T(2,128)(2,1)}), bf16[4,2,1024]{2,1,0:T(2,128)(2,1)S(1)}, u32[]{:S(2)}, u32[]{:S(2)}) async-start(bf16[4,2,1024]{2,1,0:T(2,128)(2,1)} %reshape.241), calls=%async_computation | async-start | bytes 32768 | tf_op jit(solution)/shard_map/all_to_all | solution.py:13
  23.8 6.4 %copy-start.2 = (bf16[2,64,1024]{1,2,0:T(8,128)(2,1)}, bf16[2,64,1024]{1,2,0:T(8,128)(2,1)S(1)}, u32[]{:S(2)}) copy-start(bf16[2,64,1024]{1,2,0:T(8,128)(2,1)S(1)} %copy.68) | copy-start | bytes 786436
  24.8 9.0 %all-to-all-start.4 = ((bf16[4,2,16,512]{3,2,1,0:T(8,128)(2,1)}), bf16[4,2,16,512]{3,2,1,0:T(8,128)(2,1)S(1)}, u32[]{:S(2)}, u32[]{:S(2)}) async-start(bf16[4,2,16,512]{3,2,1,0:T(8,128)(2,1)} %broadcast_in_dim.109), calls=%async_computation.4 | async-start | bytes 262144 | tf_op jit(solution)/shard_map/all_to_all | solution.py:37
  32.3 8.1 %copy-start.6 = (bf16[2,16,128]{2,1,0:T(8,128)(2,1)S(1)}, bf16[2,16,128]{2,1,0:T(8,128)(2,1)}, u32[]{:S(2)}) copy-start(bf16[2,16,128]{2,1,0:T(8,128)(2,1)} %param.28) | copy-start | bytes 24580
  33.0 7.5 %copy-start.7 = (bf16[2,16,128]{2,1,0:T(8,128)(2,1)S(1)}, bf16[2,16,128]{2,1,0:T(8,128)(2,1)}, u32[]{:S(2)}) copy-start(bf16[2,16,128]{2,1,0:T(8,128)(2,1)} %param.29) | copy-start | bytes 24580
  33.8 10.1 %all-to-all-start.1 = ((bf16[4,2,16,1024]{3,2,1,0:T(8,128)(2,1)}), bf16[4,2,16,1024]{3,2,1,0:T(8,128)(2,1)S(1)}, u32[]{:S(2)}, u32[]{:S(2)}) async-start(bf16[4,2,16,1024]{3,2,1,0:T(8,128)(2,1)} %copy.80), calls=%async_computation.1 | async-start | bytes 524288 | tf_op jit(solution)/shard_map/all_to_all | solution.py:31
  38.7 2.8 %copy-start.10 = (bf16[2,1024,128]{2,1,0:T(8,128)(2,1)S(1)}, bf16[2,1024,128]{2,1,0:T(8,128)(2,1)}, u32[]{:S(2)}) copy-start(bf16[2,1024,128]{2,1,0:T(8,128)(2,1)} %param.31) | copy-start | bytes 1572868
  41.5 2.4 %copy-start.3 = (bf16[2,16,1024]{2,1,0:T(8,128)(2,1)S(1)}, bf16[2,16,1024]{2,1,0:T(8,128)(2,1)}, u32[]{:S(2)}) copy-start(bf16[2,16,1024]{2,1,0:T(8,128)(2,1)} %param.17) | copy-start | bytes 196612
  41.5 2.4 %copy-start.4 = (bf16[2,16,1024]{2,1,0:T(8,128)(2,1)S(1)}, bf16[2,16,1024]{2,1,0:T(8,128)(2,1)}, u32[]{:S(2)}) copy-start(bf16[2,16,1024]{2,1,0:T(8,128)(2,1)} %param.18) | copy-start | bytes 196612
  41.5 2.5 %copy-start.8 = (f32[1024]{0:T(1024)S(1)}, f32[1024]{0:T(1024)}, u32[]{:S(2)}) copy-start(f32[1024]{0:T(1024)} %param.24) | copy-start | bytes 12292
  44.8 8.9 %all-to-all-start.2 = ((bf16[4,2,16,256]{3,2,1,0:T(8,128)(2,1)}), bf16[4,2,16,256]{3,2,1,0:T(8,128)(2,1)S(1)}, u32[]{:S(2)}, u32[]{:S(2)}) async-start(bf16[4,2,16,256]{3,2,1,0:T(8,128)(2,1)} %pad_maximum_fusion.2), calls=%async_computation.2 | async-start | bytes 131072 | tf_op jit(solution)/shard_map/all_to_all | solution.py:98
  53.7 10.1 %all-to-all-start.5 = ((bf16[1,2,64,520]{3,1,0,2:T(2,128)(2,1)}), bf16[1,2,64,520]{3,1,0,2:T(2,128)(2,1)S(1)}, u32[]{:S(2)}, u32[]{:S(2)}) async-start(bf16[1,2,64,520]{3,1,0,2:T(2,128)(2,1)} %pad_maximum_fusion), calls=%async_computation.5 | async-start | bytes 327680 | tf_op jit(solution)/shard_map/all_to_all | solution.py:13
  63.8 12.8 %copy-start.1 = (bf16[1,2,64,520]{3,1,0,2:T(2,128)(2,1)}, bf16[1,2,64,520]{3,1,0,2:T(2,128)(2,1)S(1)}, u32[]{:S(2)}) copy-start(bf16[1,2,64,520]{3,1,0,2:T(2,128)(2,1)S(1)} %all-to-all-done.5) | copy-start | bytes 399364
  63.8 31.1 %all-to-all-start.3 = ((bf16[32,2,2,4096]{3,1,2,0:T(2,128)(2,1)}), bf16[32,2,2,4096]{3,1,2,0:T(2,128)(2,1)S(1)}, u32[]{:S(2)}, u32[]{:S(2)}) async-start(bf16[32,2,2,4096]{3,1,2,0:T(2,128)(2,1)} %copy.82), calls=%async_computation.3 | async-start | bytes 2097152 | tf_op jit(solution)/shard_map/all_to_all | solution.py:31
